TPU v7x, 32 devices: a whole 2x2x4 slice. The times are simulated.
32 devices in a mesh: dp: 4 (over z), row: 4 (over x, core), col: 2 (over y).
Axes of the slice: x: 2, y: 2, z: 4, core: 2. Of those that a mesh axis runs over, the one named last changes fastest.
Arguments:
- tokens: bfloat16 [8, 4096, 1024], P('dp', ('row', 'col')), may hold values from -6 to 6
- cotangent: bfloat16 [8, 4096, 1024], P('dp', ('row', 'col')), may hold values from -6 to 6
- branch: int32 [8, 8], P('dp'), may hold values from 256 to 2048
- ln1_gain: float32 [1024], replicated, may hold values from 0.5 to 1.5
- ln1_bias: float32 [1024], replicated, may hold values from -1.2 to 1.2
- qkv_weight: bfloat16 [1024, 3, 1024], P('row', None, 'col'), may hold values from -0.1875 to 0.1875
- qv_bias: float32 [2, 1024], P(None, 'col'), may hold values from -1.2 to 1.2
- out_weight: bfloat16 [1024, 1024], P('col', 'row'), may hold values from -1.5 to 1.5
- out_bias: float32 [1024], replicated, may hold values from -1.2 to 1.2
- ln2_gain: float32 [1024], replicated, may hold values from 0.5 to 1.5
- ln2_bias: float32 [1024], replicated, may hold values from -1.2 to 1.2
- fc_weight: bfloat16 [1024, 4096], P('row', 'col'), may hold values from -0.1875 to 0.1875
- fc_bias: float32 [4096], P('col'), may hold values from -1.8 to 1.8
- proj_weight: bfloat16 [4096, 1024], P('col', 'row'), may hold values from -0.09375 to 0.09375
- proj_bias: float32 [1024], replicated, may hold values from -1.2 to 1.2
Outputs:
- block_out: bfloat16 [8, 4096, 1024], P('dp', ('row', 'col'))
- input_grad: float32 [8, 4096, 1024], P('dp', ('row', 'col'))
- d_ln1_gain: float32 [1024], replicated
- d_ln1_bias: float32 [1024], replicated
- d_qkv_weight: float32 [1024, 3, 1024], P(('dp', 'row'), None, 'col')
- d_qv_bias: float32 [2, 1024], replicated
- d_out_weight: float32 [1024, 1024], P('col', ('dp', 'row'))
- d_out_bias: float32 [1024], replicated
- d_ln2_gain: float32 [1024], replicated
- d_ln2_bias: float32 [1024], replicated
- d_fc_weight: float32 [1024, 4096], P(('dp', 'row'), 'col')
- d_fc_bias: float32 [4096], replicated
- d_proj_weight: float32 [4096, 1024], P('col', ('dp', 'row'))
- d_proj_bias: float32 [1024], replicated
Inputs may be any that keep to these rules, and one draw needn't show every extreme that they name: branch[g, c] is the number of leading prompt tokens that continuation c of group g sees.
All inputs are finite; a program needn't handle non-finite values.
Results may differ from a plain program's by a relative error of at most 0.015.
Values may be sent and summed in bfloat16 or wider, within the bound.
No kernel may reach another device: no remote copies, remote signals or barrier semaphores. Data moves between devices by JAX's collectives and lax.ppermute only.
A program may use at most 328 MiB of HBM per device.

v0:
```python
import jax
import jax.numpy as jnp
from jax import lax
from jax.sharding import PartitionSpec as P

HEAD = 64
PLEN = 2048
CLEN = 256
CONTS = 8
EPSILON = 1e-05
MASKED_SCORE = -1e30


def normalize(values, gain, shift):
    center = values - jnp.mean(values, axis=-1, keepdims=True)
    spread = jnp.mean(center * center, axis=-1, keepdims=True)
    return center * lax.rsqrt(spread + EPSILON) * gain + shift


def gelu_tanh(values):
    return jax.nn.gelu(values, approximate=True)


def allowed_keys(row_pos, col_pos, branch_cut):
    row_seg = jnp.where(row_pos >= PLEN, (row_pos - PLEN) // CLEN, -1)
    col_seg = jnp.where(col_pos >= PLEN, (col_pos - PLEN) // CLEN, -1)
    picked = (row_seg[:, None] == jnp.arange(CONTS, dtype=jnp.int32)[None, :]).astype(jnp.int32)
    row_cut = jnp.sum(picked * branch_cut[None, :], axis=1)
    causal = col_pos[None, :] <= row_pos[:, None]
    same_seq = col_seg[None, :] == row_seg[:, None]
    in_prefix = (
        (row_seg[:, None] >= 0) & (col_seg[None, :] < 0) & (col_pos[None, :] < row_cut[:, None])
    )
    return same_seq & causal | in_prefix


def add_trees(first, second):
    return jax.tree.map(lambda total, extra: total + extra, first, second)


def body(
    tokens,
    cotangent,
    branch,
    ln1_gain,
    ln1_bias,
    qkv_weight,
    qv_bias,
    out_weight,
    out_bias,
    ln2_gain,
    ln2_bias,
    fc_weight,
    fc_bias,
    proj_weight,
    proj_bias,
):
    scale = HEAD ** (-0.5)
    width = tokens.shape[2]
    local_rows = tokens.shape[1]
    head_cols = qv_bias.shape[1]
    head_count = head_cols // HEAD
    ff_local = fc_bias.shape[0]
    col_count = lax.axis_size("col")
    row_count = lax.axis_size("row")
    row_rows = local_rows * col_count
    group_rows = row_rows * row_count
    q_block = min(512, row_rows)
    block_count = row_rows // q_block
    row_base = lax.axis_index("row") * row_rows
    col_index = lax.axis_index("col")
    bias_three = jnp.stack([qv_bias[0], jnp.zeros_like(qv_bias[0]), qv_bias[1]])
    key_pos = jnp.arange(group_rows, dtype=jnp.int32)
    block_starts = jnp.arange(block_count, dtype=jnp.int32) * q_block

    def spread_rows(values):
        return lax.all_gather(values, "col", axis=0, tiled=True)

    def spread_grads(values):
        return lax.all_gather(values, "col", axis=0, tiled=True)

    def sum_branch(values):
        return lax.psum_scatter(values, "col", scatter_dimension=0, tiled=True)

    def sum_inputs(values):
        return lax.psum_scatter(values, "col", scatter_dimension=0, tiled=True)

    kept_weights = (
        lax.all_gather(qkv_weight, "row", axis=0, tiled=True),
        lax.all_gather(out_weight, "row", axis=1, tiled=True),
        lax.all_gather(fc_weight, "row", axis=0, tiled=True),
        lax.all_gather(proj_weight, "row", axis=1, tiled=True),
    )

    def block_scores(queries3, keys3, offset, branch_cut):
        q_part = lax.dynamic_slice_in_dim(queries3, offset, q_block, 0)
        row_pos = row_base + offset + jnp.arange(q_block, dtype=jnp.int32)
        allowed = allowed_keys(row_pos, key_pos, branch_cut)
        scores = (
            jnp.einsum("qhd,khd->hqk", q_part, keys3, preferred_element_type=jnp.float32) * scale
        )
        return (q_part, jnp.where(allowed[None], scores, MASKED_SCORE))

    def micro_step(carry, micro_item):
        grads_acc, small_acc = carry
        tok_rows, cot_rows, branch_cut = micro_item
        w_qkv, w_out, w_fc, w_proj = kept_weights
        residual = tok_rows.astype(jnp.float32)
        normed = normalize(residual, ln1_gain, ln1_bias).astype(jnp.bfloat16)
        normed_all = spread_rows(normed)
        projected = jnp.einsum("td,dsf->tsf", normed_all, w_qkv, preferred_element_type=jnp.float32)
        projected = (projected + bias_three[None]).astype(jnp.bfloat16)
        key_rows, value_rows = (
            lax.all_gather(projected[:, 1], "row", axis=0, tiled=True),
            lax.all_gather(projected[:, 2], "row", axis=0, tiled=True),
        )
        queries3 = projected[:, 0].reshape(row_rows, head_count, HEAD)
        keys3 = key_rows.reshape(group_rows, head_count, HEAD)
        values3 = value_rows.reshape(group_rows, head_count, HEAD)

        def attend(offset):
            q_part, scores = block_scores(queries3, keys3, offset, branch_cut)
            row_peak = jnp.max(scores, axis=-1, keepdims=True)
            exponent = jnp.exp(scores - row_peak)
            row_total = jnp.sum(exponent, axis=-1, keepdims=True)
            probs_low = (exponent / row_total).astype(jnp.bfloat16)
            mixed_rows = jnp.einsum(
                "hqk,khd->qhd", probs_low, values3, preferred_element_type=jnp.float32
            )
            return (mixed_rows, (row_peak + jnp.log(row_total))[..., 0])

        attended, log_totals = lax.map(attend, block_starts)
        attended = attended.reshape(row_rows, head_cols).astype(jnp.bfloat16)
        branch_part = jnp.dot(attended, w_out, preferred_element_type=jnp.float32)
        middle = residual + sum_branch(branch_part) + out_bias
        normed_two = normalize(middle, ln2_gain, ln2_bias).astype(jnp.bfloat16)
        normed_two_all = spread_rows(normed_two)
        hidden = jnp.dot(normed_two_all, w_fc, preferred_element_type=jnp.float32) + fc_bias
        active = gelu_tanh(hidden).astype(jnp.bfloat16)
        ffn_part = jnp.dot(active, w_proj, preferred_element_type=jnp.float32)
        output_rows = (middle + sum_branch(ffn_part) + proj_bias).astype(jnp.bfloat16)
        cot_all = spread_grads(cot_rows)
        grad_proj = jnp.einsum("tf,td->fd", active, cot_all, preferred_element_type=jnp.float32)
        grad_proj_bias = jnp.sum(cot_rows.astype(jnp.float32), axis=0)
        grad_active = jnp.einsum("td,fd->tf", cot_all, w_proj, preferred_element_type=jnp.float32)
        grad_hidden = jax.vjp(gelu_tanh, hidden)[1](grad_active)[0].astype(jnp.bfloat16)
        grad_fc = jnp.einsum(
            "td,tf->df", normed_two_all, grad_hidden, preferred_element_type=jnp.float32
        )
        grad_fc_bias = jnp.sum(grad_hidden.astype(jnp.float32), axis=0)
        grad_normed_two = sum_inputs(
            jnp.einsum("tf,df->td", grad_hidden, w_fc, preferred_element_type=jnp.float32)
        )
        back_middle, grad_gain_two, grad_bias_two = jax.vjp(normalize, middle, ln2_gain, ln2_bias)[
            1
        ](grad_normed_two)
        grad_middle = cot_rows.astype(jnp.float32) + back_middle
        grad_out_rows = grad_middle.astype(jnp.bfloat16)
        grad_out_all = spread_grads(grad_out_rows)
        grad_out = jnp.einsum(
            "tc,td->cd", attended, grad_out_all, preferred_element_type=jnp.float32
        )
        grad_out_bias = jnp.sum(grad_out_rows.astype(jnp.float32), axis=0)
        grad_att = jnp.einsum("td,cd->tc", grad_out_all, w_out, preferred_element_type=jnp.float32)
        grad_att = grad_att.astype(jnp.bfloat16).reshape(row_rows, head_count, HEAD)

        def attend_back(acc_pair, block_item):
            offset, log_total = block_item
            grad_keys_acc, grad_values_acc = acc_pair
            q_part, scores = block_scores(queries3, keys3, offset, branch_cut)
            probs = jnp.exp(scores - log_total[..., None])
            probs_low = probs.astype(jnp.bfloat16)
            grad_part = lax.dynamic_slice_in_dim(grad_att, offset, q_block, 0)
            grad_values_acc = grad_values_acc + jnp.einsum(
                "hqk,qhd->khd", probs_low, grad_part, preferred_element_type=jnp.float32
            )
            grad_probs = jnp.einsum(
                "qhd,khd->hqk", grad_part, values3, preferred_element_type=jnp.float32
            )
            center = jnp.sum(grad_probs * probs, axis=-1, keepdims=True)
            grad_scores = (probs * (grad_probs - center)).astype(jnp.bfloat16)
            grad_keys_acc = (
                grad_keys_acc
                + jnp.einsum(
                    "hqk,qhd->khd", grad_scores, q_part, preferred_element_type=jnp.float32
                )
                * scale
            )
            grad_query = (
                jnp.einsum("hqk,khd->qhd", grad_scores, keys3, preferred_element_type=jnp.float32)
                * scale
            )
            return ((grad_keys_acc, grad_values_acc), grad_query)

        empty_keys = jnp.zeros((group_rows, head_count, HEAD), jnp.float32)
        (grad_keys, grad_values), grad_queries = lax.scan(
            attend_back, (empty_keys, empty_keys), (block_starts, log_totals)
        )
        own_keys, own_values = (
            lax.psum_scatter(
                grad_keys.reshape(group_rows, head_cols).astype(jnp.bfloat16),
                "row",
                scatter_dimension=0,
                tiled=True,
            ).astype(jnp.float32),
            lax.psum_scatter(
                grad_values.reshape(group_rows, head_cols).astype(jnp.bfloat16),
                "row",
                scatter_dimension=0,
                tiled=True,
            ).astype(jnp.float32),
        )
        grad_projected = jnp.stack(
            [grad_queries.reshape(row_rows, head_cols), own_keys, own_values], axis=1
        ).astype(jnp.bfloat16)
        grad_qkv = jnp.einsum(
            "td,tsf->dsf", normed_all, grad_projected, preferred_element_type=jnp.float32
        )
        grad_qkv_bias = jnp.sum(grad_projected.astype(jnp.float32), axis=0)
        grad_normed = sum_inputs(
            jnp.einsum("tsf,dsf->td", grad_projected, w_qkv, preferred_element_type=jnp.float32)
        )
        back_input, grad_gain_one, grad_bias_one = jax.vjp(normalize, residual, ln1_gain, ln1_bias)[
            1
        ](grad_normed)
        input_rows = grad_middle + back_input
        weight_terms = (grad_qkv, grad_out, grad_fc, grad_proj)
        small_terms = (
            grad_gain_one,
            grad_bias_one,
            grad_qkv_bias,
            grad_out_bias,
            grad_gain_two,
            grad_bias_two,
            grad_fc_bias,
            grad_proj_bias,
        )
        return (
            (add_trees(grads_acc, weight_terms), add_trees(small_acc, small_terms)),
            (output_rows, input_rows),
        )

    grads_init = (
        jnp.zeros((width, 3, head_cols), jnp.float32),
        jnp.zeros((head_cols, width), jnp.float32),
        jnp.zeros((width, ff_local), jnp.float32),
        jnp.zeros((ff_local, width), jnp.float32),
    )
    vector_zero = jnp.zeros((width,), jnp.float32)
    small_init = (
        vector_zero,
        vector_zero,
        jnp.zeros((3, head_cols), jnp.float32),
        vector_zero,
        vector_zero,
        vector_zero,
        jnp.zeros((ff_local,), jnp.float32),
        vector_zero,
    )
    (grads_acc, small_acc), (block_out, input_grad) = lax.scan(
        micro_step, (grads_init, small_init), (tokens, cotangent, branch)
    )
    (
        gain_one,
        bias_one,
        qkv_bias_acc,
        out_bias_acc,
        gain_two,
        bias_two,
        fc_bias_acc,
        proj_bias_acc,
    ) = small_acc
    qv_full = lax.dynamic_update_slice(
        jnp.zeros((2, width), jnp.float32),
        jnp.stack([qkv_bias_acc[0], qkv_bias_acc[2]]),
        (jnp.int32(0), col_index * head_cols),
    )
    fc_full = lax.dynamic_update_slice(
        jnp.zeros((ff_local * col_count,), jnp.float32), fc_bias_acc, (col_index * ff_local,)
    )
    summed = lax.psum(
        (gain_one, bias_one, qv_full, out_bias_acc, gain_two, bias_two, fc_full, proj_bias_acc),
        ("dp", "row", "col"),
    )
    return (
        block_out,
        input_grad,
        summed[0],
        summed[1],
        lax.psum_scatter(
            grads_acc[0].astype(jnp.bfloat16), ("dp", "row"), scatter_dimension=0, tiled=True
        ).astype(jnp.float32),
        summed[2],
        lax.psum_scatter(
            grads_acc[1].astype(jnp.bfloat16), ("dp", "row"), scatter_dimension=1, tiled=True
        ).astype(jnp.float32),
        summed[3],
        summed[4],
        summed[5],
        lax.psum_scatter(
            grads_acc[2].astype(jnp.bfloat16), ("dp", "row"), scatter_dimension=0, tiled=True
        ).astype(jnp.float32),
        summed[6],
        lax.psum_scatter(
            grads_acc[3].astype(jnp.bfloat16), ("dp", "row"), scatter_dimension=1, tiled=True
        ).astype(jnp.float32),
        summed[7],
    )


def solution(mesh):
    placed = (
        P("dp", ("row", "col"), None),
        P("dp", ("row", "col"), None),
        P("dp", None),
        P(),
        P(),
        P("row", None, "col"),
        P(None, "col"),
        P("col", "row"),
        P(),
        P(),
        P(),
        P("row", "col"),
        P("col"),
        P("col", "row"),
        P(),
    )
    return jax.shard_map(
        body,
        mesh=mesh,
        in_specs=placed,
        out_specs=(
            P("dp", ("row", "col"), None),
            P("dp", ("row", "col"), None),
            P(),
            P(),
            P(("dp", "row"), None, "col"),
            P(),
            P("col", ("dp", "row")),
            P(),
            P(),
            P(),
            P(("dp", "row"), "col"),
            P(),
            P("col", ("dp", "row")),
            P(),
        ),
        check_vma=False,
    )
```

profile of v0, /device:TPU:0, one launch (start us, length us, event | category | flops | bytes accessed | tf_op | source)
XLA Modules:
  0.0 2760.7 jit_solution(3911327315650754905)
XLA Ops:
  131.7 2337.8 %while.107 = (s32[]{:T(128)}, f32[1024,3,512]{2,0,1:T(8,128)}, f32[512,1024]{1,0:T(8,128)}, f32[1024,2048]{1,0:T(8,128)}, f32[2048,1024]{1,0:T(8,128)}, /*index=...) while((s32[]{:T(128)}, f32[1024,3,512]{2,0,1:T(8,128)}, ...), condition=%wide.region_32.33_spmd.clone.clone, body=%wide.region_0.32_spmd.clone.clone.sunk | while | flops 54250668032 | bytes 1470284544 | solution.py:260
  251.0 166.1 %while.108 = (s32[]{:T(128)}, bf16[2,512,8,64]{1,3,2,0:T(8,128)(2,1)}, f32[2,8,512]{2,1,0:T(8,128)S(1)}, s32[4096]{0:T(1024)S(1)}, s32[2]{0:T(128)S(1)}, /*index...) while((s32[]{:T(128)}, ...), condition=%wide.region_7.7_spmd.clone, body=%wide.region_3.6_spmd.clone.sunk | while | flops 4511079424 | bytes 219897072 | solution.py:132
  424.1 54.5 %reduce-scatter.19.cloned.1.call-done = f32[512,1024]{1,0:T(8,128)} async-done(((f32[1024,1024]{1,0:T(8,128)}), f32[512,1024]{1,0:T(8,128)}) %reduce-scatter.19.cloned.1.call-update) | async-done | bytes 2097168 | tf_op jit(solution)/shard_map/while/body/eval_jaxpr/reduce_scatter | solution.py:83
  572.4 54.5 %reduce-scatter.21.cloned.1.call-done = f32[512,1024]{1,0:T(8,128)} async-done(((f32[1024,1024]{1,0:T(8,128)}), f32[512,1024]{1,0:T(8,128)}) %reduce-scatter.21.cloned.1.call-update) | async-done | bytes 2097168 | tf_op jit(solution)/shard_map/while/body/eval_jaxpr/reduce_scatter | solution.py:86
  672.4 396.0 %while.109 = (s32[]{:T(128)}, f32[4096,8,64]{0,2,1:T(8,128)}, f32[4096,8,64]{0,2,1:T(8,128)}, bf16[2,512,8,64]{1,3,2,0:T(8,128)(2,1)}, s32[2]{0:T(128)S(1)}, /*i...) while((s32[]{:T(128)}, f32[4096,8,64]{0,2,1:T(8,128)}, ...), condition=%wide.region_17.17_spmd.clone.clone, body=%wide.region_14.16_spmd.clone.clone.sunk | while | flops 10913946624 | bytes 590913280 | solution.py:196
  734.5 43.6 %multiply_reduce_fusion.9 = (f32[8,512]{1,0:T(8,128)S(1)}, f32[8,512,4096]{2,1,0:T(8,128)}) fusion(f32[8,512,4096]{2,1,0:T(8,128)} %subtract_exponential_fusion.3, bf16[4096,8,64]{0,2,1:T(8,128)(2,1)S(1)} %copy-done, bf16[1024,8,64]{0,2,1:T(8,128)(2,1)} %get-tuple-element.1915, s32[]{:T(128)S(6)} %select_n.260), kind=kOutput, calls=%fused_computation.39.clone.2 | convolution fusion | flops 2181033984 | bytes 138952704 | tf_op jit(solution)/shard_map/while/body/eval_jaxpr/while/body/eval_jaxpr/qhd,khd->hqk/dot_general | solution.py:177
  778.1 53.0 %multiply_convert_fusion.9 = bf16[8,512,4096]{2,1,0:T(8,128)(2,1)} fusion(f32[8,512,4096]{2,1,0:T(8,128)} %subtract_exponential_fusion.3, f32[8,512,4096]{2,1,0:T(8,128)} %get-tuple-element.1831, f32[8,512]{1,0:T(8,128)S(1)} %get-tuple-element.1832), kind=kLoop, calls=%fused_computation.38.clone.1 | loop fusion | flops 50331648 | bytes 167788544 | tf_op jit(solution)/shard_map/while/body/eval_jaxpr/while/body/eval_jaxpr/convert_element_type | solution.py:181
  932.2 43.6 %multiply_reduce_fusion.9 = (f32[8,512]{1,0:T(8,128)S(1)}, f32[8,512,4096]{2,1,0:T(8,128)}) fusion(f32[8,512,4096]{2,1,0:T(8,128)} %subtract_exponential_fusion.3, bf16[4096,8,64]{0,2,1:T(8,128)(2,1)S(1)} %copy-done, bf16[1024,8,64]{0,2,1:T(8,128)(2,1)} %get-tuple-element.1915, s32[]{:T(128)S(6)} %select_n.260), kind=kOutput, calls=%fused_computation.39.clone.2 | convolution fusion | flops 2181033984 | bytes 138952704 | tf_op jit(solution)/shard_map/while/body/eval_jaxpr/while/body/eval_jaxpr/qhd,khd->hqk/dot_general | solution.py:177
  975.8 53.0 %multiply_convert_fusion.9 = bf16[8,512,4096]{2,1,0:T(8,128)(2,1)} fusion(f32[8,512,4096]{2,1,0:T(8,128)} %subtract_exponential_fusion.3, f32[8,512,4096]{2,1,0:T(8,128)} %get-tuple-element.1831, f32[8,512]{1,0:T(8,128)S(1)} %get-tuple-element.1832), kind=kLoop, calls=%fused_computation.38.clone.1 | loop fusion | flops 50331648 | bytes 167788544 | tf_op jit(solution)/shard_map/while/body/eval_jaxpr/while/body/eval_jaxpr/convert_element_type | solution.py:181
  1125.6 47.0 %reduce-scatter.23.cloned.1.call-done = bf16[1024,512]{1,0:T(8,128)(2,1)} async-done(((bf16[4096,512]{1,0:T(8,128)(2,1)}), bf16[1024,512]{1,0:T(8,128)(2,1)}) %reduce-scatter.23.cloned.1.call-update) | async-done | bytes 1048592 | tf_op jit(solution)/shard_map/while/body/eval_jaxpr/reduce_scatter | solution.py:206
  1241.5 44.2 %reduce-scatter.27.cloned.1.call-done = f32[512,1024]{1,0:T(8,128)} async-done(((f32[1024,1024]{1,0:T(8,128)}), f32[512,1024]{1,0:T(8,128)}) %reduce-scatter.27.cloned.1.call-update) | async-done | bytes 2097168 | tf_op jit(solution)/shard_map/while/body/eval_jaxpr/reduce_scatter | solution.py:86
  1412.5 177.5 %while.108 = (s32[]{:T(128)}, bf16[2,512,8,64]{1,3,2,0:T(8,128)(2,1)}, f32[2,8,512]{2,1,0:T(8,128)S(1)}, s32[4096]{0:T(1024)S(1)}, s32[2]{0:T(128)S(1)}, /*index...) while((s32[]{:T(128)}, ...), condition=%wide.region_7.7_spmd.clone, body=%wide.region_3.6_spmd.clone.sunk | while | flops 4511079424 | bytes 219897072 | solution.py:132
  1597.1 54.5 %reduce-scatter.19.cloned.1.call-done = f32[512,1024]{1,0:T(8,128)} async-done(((f32[1024,1024]{1,0:T(8,128)}), f32[512,1024]{1,0:T(8,128)}) %reduce-scatter.19.cloned.1.call-update) | async-done | bytes 2097168 | tf_op jit(solution)/shard_map/while/body/eval_jaxpr/reduce_scatter | solution.py:83
  1745.5 54.5 %reduce-scatter.21.cloned.1.call-done = f32[512,1024]{1,0:T(8,128)} async-done(((f32[1024,1024]{1,0:T(8,128)}), f32[512,1024]{1,0:T(8,128)}) %reduce-scatter.21.cloned.1.call-update) | async-done | bytes 2097168 | tf_op jit(solution)/shard_map/while/body/eval_jaxpr/reduce_scatter | solution.py:86
  1845.5 396.0 %while.109 = (s32[]{:T(128)}, f32[4096,8,64]{0,2,1:T(8,128)}, f32[4096,8,64]{0,2,1:T(8,128)}, bf16[2,512,8,64]{1,3,2,0:T(8,128)(2,1)}, s32[2]{0:T(128)S(1)}, /*i...) while((s32[]{:T(128)}, f32[4096,8,64]{0,2,1:T(8,128)}, ...), condition=%wide.region_17.17_spmd.clone.clone, body=%wide.region_14.16_spmd.clone.clone.sunk | while | flops 10913946624 | bytes 590913280 | solution.py:196
  1907.8 43.6 %multiply_reduce_fusion.9 = (f32[8,512]{1,0:T(8,128)S(1)}, f32[8,512,4096]{2,1,0:T(8,128)}) fusion(f32[8,512,4096]{2,1,0:T(8,128)} %subtract_exponential_fusion.3, bf16[4096,8,64]{0,2,1:T(8,128)(2,1)S(1)} %copy-done, bf16[1024,8,64]{0,2,1:T(8,128)(2,1)} %get-tuple-element.1915, s32[]{:T(128)S(6)} %select_n.260), kind=kOutput, calls=%fused_computation.39.clone.2 | convolution fusion | flops 2181033984 | bytes 138952704 | tf_op jit(solution)/shard_map/while/body/eval_jaxpr/while/body/eval_jaxpr/qhd,khd->hqk/dot_general | solution.py:177
  1951.4 53.0 %multiply_convert_fusion.9 = bf16[8,512,4096]{2,1,0:T(8,128)(2,1)} fusion(f32[8,512,4096]{2,1,0:T(8,128)} %subtract_exponential_fusion.3, f32[8,512,4096]{2,1,0:T(8,128)} %get-tuple-element.1831, f32[8,512]{1,0:T(8,128)S(1)} %get-tuple-element.1832), kind=kLoop, calls=%fused_computation.38.clone.1 | loop fusion | flops 50331648 | bytes 167788544 | tf_op jit(solution)/shard_map/while/body/eval_jaxpr/while/body/eval_jaxpr/convert_element_type | solution.py:181
  2105.6 43.6 %multiply_reduce_fusion.9 = (f32[8,512]{1,0:T(8,128)S(1)}, f32[8,512,4096]{2,1,0:T(8,128)}) fusion(f32[8,512,4096]{2,1,0:T(8,128)} %subtract_exponential_fusion.3, bf16[4096,8,64]{0,2,1:T(8,128)(2,1)S(1)} %copy-done, bf16[1024,8,64]{0,2,1:T(8,128)(2,1)} %get-tuple-element.1915, s32[]{:T(128)S(6)} %select_n.260), kind=kOutput, calls=%fused_computation.39.clone.2 | convolution fusion | flops 2181033984 | bytes 138952704 | tf_op jit(solution)/shard_map/while/body/eval_jaxpr/while/body/eval_jaxpr/qhd,khd->hqk/dot_general | solution.py:177
  2149.1 53.0 %multiply_convert_fusion.9 = bf16[8,512,4096]{2,1,0:T(8,128)(2,1)} fusion(f32[8,512,4096]{2,1,0:T(8,128)} %subtract_exponential_fusion.3, f32[8,512,4096]{2,1,0:T(8,128)} %get-tuple-element.1831, f32[8,512]{1,0:T(8,128)S(1)} %get-tuple-element.1832), kind=kLoop, calls=%fused_computation.38.clone.1 | loop fusion | flops 50331648 | bytes 167788544 | tf_op jit(solution)/shard_map/while/body/eval_jaxpr/while/body/eval_jaxpr/convert_element_type | solution.py:181
  2298.7 47.0 %reduce-scatter.23.cloned.1.call-done = bf16[1024,512]{1,0:T(8,128)(2,1)} async-done(((bf16[4096,512]{1,0:T(8,128)(2,1)}), bf16[1024,512]{1,0:T(8,128)(2,1)}) %reduce-scatter.23.cloned.1.call-update) | async-done | bytes 1048592 | tf_op jit(solution)/shard_map/while/body/eval_jaxpr/reduce_scatter | solution.py:206
  2416.9 42.1 %reduce-scatter.27.cloned.1.call-done = f32[512,1024]{1,0:T(8,128)} async-done(((f32[1024,1024]{1,0:T(8,128)}), f32[512,1024]{1,0:T(8,128)}) %reduce-scatter.27.cloned.1.call-update) | async-done | bytes 2097168 | tf_op jit(solution)/shard_map/while/body/eval_jaxpr/reduce_scatter | solution.py:86
  2534.1 66.8 %reduce-scatter.11.cloned.1.call-done = bf16[64,3,512]{2,0,1:T(8,128)(2,1)} async-done(((bf16[1024,3,512]{2,0,1:T(8,128)(2,1)}), bf16[64,3,512]{2,0,1:T(8,128)(2,1)}) %reduce-scatter.11.cloned.1.call-update) | async-done | bytes 196624 | tf_op jit(solution)/shard_map/reduce_scatter | solution.py:290
  2602.6 73.7 %reduce-scatter.15.cloned.1.call-done = bf16[64,2048]{1,0:T(8,128)(2,1)} async-done(((bf16[1024,2048]{1,0:T(8,128)(2,1)}), bf16[64,2048]{1,0:T(8,128)(2,1)}) %reduce-scatter.15.cloned.1.call-update) | async-done | bytes 262160 | tf_op jit(solution)/shard_map/reduce_scatter | solution.py:300
  2678.2 73.9 %reduce-scatter.17.cloned.1.call-done = bf16[2048,64]{0,1:T(8,128)(2,1)} async-done(((bf16[2048,1024]{0,1:T(8,128)(2,1)}), bf16[2048,64]{0,1:T(8,128)(2,1)}) %reduce-scatter.17.cloned.1.call-update) | async-done | bytes 262160 | tf_op jit(solution)/shard_map/reduce_scatter | solution.py:304
  (692 shorter events, 1707.7 us)
Async XLA Ops:
  8.7 86.6 %all-gather.29.cloned.1.call-start = ((), (), s32[]{:S(2)}) async-start(), calls=%async_computation.13 | async-start | bytes 5242880 | tf_op jit(solution)/shard_map/all_gather | solution.py:91
  9.4 122.3 %all-gather.25.cloned.1.call-start = ((), (), s32[]{:S(2)}) async-start(), calls=%async_computation.11 | async-start | bytes 5242880 | tf_op jit(solution)/shard_map/all_gather | solution.py:92
  138.8 75.0 %all-gather.33.cloned.1.call-start = ((), (), s32[]{:S(2)}) async-start(), calls=%async_computation.19 | async-start | bytes 5242880 | tf_op jit(solution)/shard_map/while/body/eval_jaxpr/all_gather | solution.py:114
  179.9 298.6 %reduce-scatter.19.cloned.1.call-start = ((), (), s32[]{:S(2)}) async-start(), calls=%async_computation.21 | async-start | bytes 6291456 | tf_op jit(solution)/shard_map/while/body/eval_jaxpr/reduce_scatter | solution.py:83
  424.1 91.8 %all-gather.37.cloned.1.call-start = ((), (), s32[]{:S(2)}) async-start(), calls=%async_computation.22 | async-start | bytes 3145728 | tf_op jit(solution)/shard_map/while/body/eval_jaxpr/all_gather | solution.py:77
  485.7 141.2 %reduce-scatter.21.cloned.1.call-start = ((), (), s32[]{:S(2)}) async-start(), calls=%async_computation.24 | async-start | bytes 6291456 | tf_op jit(solution)/shard_map/while/body/eval_jaxpr/reduce_scatter | solution.py:86
  572.4 95.0 %all-gather.41.cloned.1.call-start = ((), (), s32[]{:S(2)}) async-start(), calls=%async_computation.25 | async-start | bytes 3145728 | tf_op jit(solution)/shard_map/while/body/eval_jaxpr/all_gather | solution.py:80
  634.1 491.5 %reduce-scatter.25.cloned.1.call-start = ((), (), s32[]{:S(2)}) async-start(), calls=%async_computation.27 | async-start | bytes 5242880 | tf_op jit(solution)/shard_map/while/body/eval_jaxpr/reduce_scatter | solution.py:200
  1080.9 91.7 %reduce-scatter.23.cloned.1.call-start = ((), (), s32[]{:S(2)}) async-start(), calls=%async_computation.26 | async-start | bytes 5242880 | tf_op jit(solution)/shard_map/while/body/eval_jaxpr/reduce_scatter | solution.py:206
  1093.8 135.4 %reduce-scatter.29.cloned.1.call-start = ((), (), s32[]{:S(2)}) async-start(), calls=%async_computation.29 | async-start | bytes 6291456 | tf_op jit(solution)/shard_map/while/body/eval_jaxpr/reduce_scatter | solution.py:83
  1106.4 179.4 %reduce-scatter.27.cloned.1.call-start = ((), (), s32[]{:S(2)}) async-start(), calls=%async_computation.28 | async-start | bytes 6291456 | tf_op jit(solution)/shard_map/while/body/eval_jaxpr/reduce_scatter | solution.py:86
  1300.4 75.0 %all-gather.33.cloned.1.call-start = ((), (), s32[]{:S(2)}) async-start(), calls=%async_computation.19 | async-start | bytes 5242880 | tf_op jit(solution)/shard_map/while/body/eval_jaxpr/all_gather | solution.py:114
  1340.7 70.7 %all-gather.35.cloned.1.call-start = ((), (), s32[]{:S(2)}) async-start(), calls=%async_computation.20 | async-start | bytes 5242880 | tf_op jit(solution)/shard_map/while/body/eval_jaxpr/all_gather | solution.py:115
  1341.5 310.0 %reduce-scatter.19.cloned.1.call-start = ((), (), s32[]{:S(2)}) async-start(), calls=%async_computation.21 | async-start | bytes 6291456 | tf_op jit(solution)/shard_map/while/body/eval_jaxpr/reduce_scatter | solution.py:83
  1597.0 91.8 %all-gather.37.cloned.1.call-start = ((), (), s32[]{:S(2)}) async-start(), calls=%async_computation.22 | async-start | bytes 3145728 | tf_op jit(solution)/shard_map/while/body/eval_jaxpr/all_gather | solution.py:77
  1658.6 141.4 %reduce-scatter.21.cloned.1.call-start = ((), (), s32[]{:S(2)}) async-start(), calls=%async_computation.24 | async-start | bytes 6291456 | tf_op jit(solution)/shard_map/while/body/eval_jaxpr/reduce_scatter | solution.py:86
  1745.5 95.0 %all-gather.41.cloned.1.call-start = ((), (), s32[]{:S(2)}) async-start(), calls=%async_computation.25 | async-start | bytes 3145728 | tf_op jit(solution)/shard_map/while/body/eval_jaxpr/all_gather | solution.py:80
  1807.2 491.5 %reduce-scatter.25.cloned.1.call-start = ((), (), s32[]{:S(2)}) async-start(), calls=%async_computation.27 | async-start | bytes 5242880 | tf_op jit(solution)/shard_map/while/body/eval_jaxpr/reduce_scatter | solution.py:200
  2254.0 91.7 %reduce-scatter.23.cloned.1.call-start = ((), (), s32[]{:S(2)}) async-start(), calls=%async_computation.26 | async-start | bytes 5242880 | tf_op jit(solution)/shard_map/while/body/eval_jaxpr/reduce_scatter | solution.py:206
  2266.9 135.4 %reduce-scatter.29.cloned.1.call-start = ((), (), s32[]{:S(2)}) async-start(), calls=%async_computation.29 | async-start | bytes 6291456 | tf_op jit(solution)/shard_map/while/body/eval_jaxpr/reduce_scatter | solution.py:83
  2279.5 179.5 %reduce-scatter.27.cloned.1.call-start = ((), (), s32[]{:S(2)}) async-start(), calls=%async_computation.28 | async-start | bytes 6291456 | tf_op jit(solution)/shard_map/while/body/eval_jaxpr/reduce_scatter | solution.py:86
  2472.2 128.7 %reduce-scatter.11.cloned.1.call-start = ((), (), s32[]{:S(2)}) async-start(), calls=%async_computation.14 | async-start | bytes 3342336 | tf_op jit(solution)/shard_map/reduce_scatter | solution.py:290
  2477.1 199.3 %reduce-scatter.15.cloned.1.call-start = ((), (), s32[]{:S(2)}) async-start(), calls=%async_computation.16 | async-start | bytes 4456448 | tf_op jit(solution)/shard_map/reduce_scatter | solution.py:300
  2483.2 268.8 %reduce-scatter.17.cloned.1.call-start = ((), (), s32[]{:S(2)}) async-start(), calls=%async_computation.17 | async-start | bytes 4456448 | tf_op jit(solution)/shard_map/reduce_scatter | solution.py:304
  (196 other events, 4598.0 us)
Sparse Core Ops, SparseCore 0:
  60.8 34.4 all-gather.28
  96.7 34.9 all-gather.24
  179.3 34.4 all-gather.32
  215.3 34.4 all-gather.34
  424.2 54.3 reduce-scatter.18
  482.7 33.0 all-gather.36
  572.5 54.3 reduce-scatter.20
  634.2 33.0 all-gather.40
  1081.0 44.5 reduce-scatter.24
  1128.0 44.5 reduce-scatter.22
  1174.7 54.3 reduce-scatter.28
  1231.3 54.3 reduce-scatter.26
  1340.9 34.4 all-gather.32
  1376.9 34.4 all-gather.34
  1597.1 54.3 reduce-scatter.18
  1745.6 54.3 reduce-scatter.20
  2254.1 44.5 reduce-scatter.24
  2301.1 44.5 reduce-scatter.22
  2347.9 54.3 reduce-scatter.28
  2404.6 54.3 reduce-scatter.26
  2474.0 57.7 reduce-scatter.12
  2535.4 65.4 reduce-scatter.10
  2604.8 71.5 reduce-scatter.14
  2680.2 71.7 reduce-scatter.16
  (8 shorter events, 246.1 us)
where the time goes:
time: 2770 us; the launch traced here: 2760 us
  waiting for transfers between devices  1190 us (43%)
  matrix products  959 us (35%)
  other arithmetic  432 us (16%)
  local copies, waits for them, and re-layouts  83 us (3%)
  blocking collectives  40.9 us (1%)
  loops' own time  39.9 us (1%)
    dot_general x8, matrix products, block_scores(): jnp.einsum('qhd,khd->hqk', q_part, keys3, preferred_element_type=jnp.floa...  219 us
    convert_element_type x4, other arithmetic, attend_back(): grad_scores = (probs * (grad_probs - center)).astype(jnp.bfloat16)  212 us
    reduce_scatter x4, waiting for transfers between devices, sum_inputs(): return lax.psum_scatter(values, 'col', scatter_dimension=0, tiled=True)  195 us
    dot_general x4, matrix products, attend_back(): jnp.einsum('qhd,khd->hqk', grad_part, values3, preferred_element_type=jnp...  174 us
    reduce_scatter x4, waiting for transfers between devices, sum_branch(): return lax.psum_scatter(values, 'col', scatter_dimension=0, tiled=True)  152 us
    all_gather x4, waiting for transfers between devices, spread_rows(): return lax.all_gather(values, 'col', axis=0, tiled=True)  127 us
    all_gather x4, waiting for transfers between devices, spread_grads(): return lax.all_gather(values, 'col', axis=0, tiled=True)  114 us
    dot_general x4, matrix products, attend(): jnp.einsum('hqk,khd->qhd', probs_low, values3, preferred_element_type=jnp...  111 us
  transfers between devices with their start and end apart: 32, of which 31 were waited for; matrix products, arithmetic and copies ran while one was open for 7% of the time, Pallas kernels for 0%

commit v1 on v0

--- a/solution.py
+++ b/solution.py
@@ -2,6 +2,7 @@
 import jax.numpy as jnp
 from jax import lax
 from jax.sharding import PartitionSpec as P
+from jax.lax import axis_index, axis_size, ppermute
 
 HEAD = 64
 PLEN = 2048
@@ -9,6 +10,25 @@
 CONTS = 8
 EPSILON = 1e-05
 MASKED_SCORE = -1e30
+
+
+def _update_samples_all(my_data, link_axis, dim_at):
+    carry_out, frame_out, y = (axis_size(link_axis), axis_index(link_axis), my_data.shape[dim_at])
+    all_values, o_now = (my_data, 1)
+    while o_now < carry_out:
+        all_values = jnp.concatenate(
+            [
+                all_values,
+                ppermute(
+                    all_values,
+                    axis_name=link_axis,
+                    perm=[(d, (d - o_now) % carry_out) for d in range(carry_out)],
+                ),
+            ],
+            axis=dim_at,
+        )
+        o_now = 2 * o_now
+    return jnp.roll(all_values, frame_out * y, axis=dim_at)
 
 
 def normalize(values, gain, shift):
@@ -111,7 +131,7 @@
         projected = jnp.einsum("td,dsf->tsf", normed_all, w_qkv, preferred_element_type=jnp.float32)
         projected = (projected + bias_three[None]).astype(jnp.bfloat16)
         key_rows, value_rows = (
-            lax.all_gather(projected[:, 1], "row", axis=0, tiled=True),
+            _update_samples_all(projected[:, 1], link_axis="row", dim_at=0),
             lax.all_gather(projected[:, 2], "row", axis=0, tiled=True),
         )
         queries3 = projected[:, 0].reshape(row_rows, head_count, HEAD)

time: 2770 us -> 2790 us (level)
    ppermute x0 -> x4, waiting for transfers between devices: none -> 156 us  [_update_samples_all(): ppermute(all_values, axis_name=link_axis, perm=[(d, (d - o_now) % carry_o...]
    all_gather x2, waiting for transfers between devices: 72.1 us -> 0.01 us  [micro_step(): lax.all_gather(projected[:, 2], 'row', axis=0, tiled=True)]
    all_gather x2 -> x0, waiting for transfers between devices: 67 us -> none  [micro_step(): lax.all_gather(projected[:, 1], 'row', axis=0, tiled=True)]
  transfers between devices with their start and end apart: 32 -> 34, of which waited for: 31 -> 31; matrix products, arithmetic and copies ran while one was open for 7% -> 8% of each run, Pallas kernels for 0% -> 0%
where the time goes in v1:
time: 2790 us
  waiting for transfers between devices  1200 us (43%)
  matrix products  960 us (34%)
  other arithmetic  435 us (16%)
  local copies, waits for them, and re-layouts  103 us (4%)
  blocking collectives  40.9 us (1%)
  loops' own time  28.9 us (1%)
    dot_general x8, matrix products, block_scores(): jnp.einsum('qhd,khd->hqk', q_part, keys3, preferred_element_type=jnp.floa...  219 us
    convert_element_type x4, other arithmetic, attend_back(): grad_scores = (probs * (grad_probs - center)).astype(jnp.bfloat16)  212 us
    reduce_scatter x4, waiting for transfers between devices, sum_inputs(): return lax.psum_scatter(values, 'col', scatter_dimension=0, tiled=True)  195 us
    dot_general x4, matrix products, attend_back(): jnp.einsum('qhd,khd->hqk', grad_part, values3, preferred_element_type=jnp...  174 us
    ppermute x4, waiting for transfers between devices, _update_samples_all(): ppermute(all_values, axis_name=link_axis, perm=[(d, (d - o_now) % carry_o...  156 us
    reduce_scatter x4, waiting for transfers between devices, sum_branch(): return lax.psum_scatter(values, 'col', scatter_dimension=0, tiled=True)  151 us
    all_gather x4, waiting for transfers between devices, spread_rows(): return lax.all_gather(values, 'col', axis=0, tiled=True)  127 us
    all_gather x4, waiting for transfers between devices, spread_grads(): return lax.all_gather(values, 'col', axis=0, tiled=True)  114 us
  transfers between devices with their start and end apart: 34, of which 31 were waited for; matrix products, arithmetic and copies ran while one was open for 8% of the time, Pallas kernels for 0%

profile of v1, /device:TPU:0, one launch (start us, length us, event | category | flops | bytes accessed | tf_op | source)
XLA Modules:
  0.0 2788.6 jit_solution(6670517563155471712)
XLA Ops:
  131.7 2365.6 %while.107 = (s32[]{:T(128)}, f32[1024,3,512]{2,0,1:T(8,128)}, f32[512,1024]{1,0:T(8,128)}, f32[1024,2048]{1,0:T(8,128)}, f32[2048,1024]{1,0:T(8,128)}, /*index=...) while((s32[]{:T(128)}, f32[1024,3,512]{2,0,1:T(8,128)}, ...), condition=%wide.region_32.33_spmd.clone.clone, body=%wide.region_0.32_spmd.clone.clone.sunk | while | flops 54254862336 | bytes 1509082112 | solution.py:280
  206.1 56.3 %collective-permute-done.1 = bf16[2048,512]{0,1:T(8,128)(2,1)} collective-permute-done((bf16[2048,512]{0,1:T(8,128)(2,1)}, bf16[2048,512]{0,1:T(8,128)(2,1)}, u32[]{:S(2)}, u32[]{:S(2)}) %collective-permute-start.1) | collective-permute-done | bytes 2097184 | tf_op jit(solution)/shard_map/while/body/eval_jaxpr/ppermute | solution.py:22
  270.6 166.4 %while.108 = (s32[]{:T(128)}, bf16[2,512,8,64]{1,3,2,0:T(8,128)(2,1)}, f32[2,8,512]{2,1,0:T(8,128)S(1)}, s32[4096]{0:T(1024)S(1)}, s32[2]{0:T(128)S(1)}, /*index...) while((s32[]{:T(128)}, ...), condition=%wide.region_7.7_spmd.clone, body=%wide.region_3.6_spmd.clone.sunk | while | flops 4511079424 | bytes 219897072 | solution.py:152
  444.1 53.8 %reduce-scatter.19.cloned.1.call-done = f32[512,1024]{1,0:T(8,128)} async-done(((f32[1024,1024]{1,0:T(8,128)}), f32[512,1024]{1,0:T(8,128)}) %reduce-scatter.19.cloned.1.call-update) | async-done | bytes 2097168 | tf_op jit(solution)/shard_map/while/body/eval_jaxpr/reduce_scatter | solution.py:103
  592.0 54.5 %reduce-scatter.21.cloned.1.call-done = f32[512,1024]{1,0:T(8,128)} async-done(((f32[1024,1024]{1,0:T(8,128)}), f32[512,1024]{1,0:T(8,128)}) %reduce-scatter.21.cloned.1.call-update) | async-done | bytes 2097168 | tf_op jit(solution)/shard_map/while/body/eval_jaxpr/reduce_scatter | solution.py:106
  692.0 396.0 %while.109 = (s32[]{:T(128)}, f32[4096,8,64]{0,2,1:T(8,128)}, f32[4096,8,64]{0,2,1:T(8,128)}, bf16[2,512,8,64]{1,3,2,0:T(8,128)(2,1)}, s32[2]{0:T(128)S(1)}, /*i...) while((s32[]{:T(128)}, f32[4096,8,64]{0,2,1:T(8,128)}, ...), condition=%wide.region_17.17_spmd.clone.clone, body=%wide.region_14.16_spmd.clone.clone.sunk | while | flops 10913946624 | bytes 590913280 | solution.py:216
  754.1 43.6 %multiply_reduce_fusion.9 = (f32[8,512]{1,0:T(8,128)S(1)}, f32[8,512,4096]{2,1,0:T(8,128)}) fusion(f32[8,512,4096]{2,1,0:T(8,128)} %subtract_exponential_fusion.3, bf16[4096,8,64]{0,2,1:T(8,128)(2,1)S(1)} %copy-done, bf16[1024,8,64]{0,2,1:T(8,128)(2,1)} %get-tuple-element.1924, s32[]{:T(128)S(6)} %select_n.291), kind=kOutput, calls=%fused_computation.39.clone.2 | convolution fusion | flops 2181033984 | bytes 138952704 | tf_op jit(solution)/shard_map/while/body/eval_jaxpr/while/body/eval_jaxpr/qhd,khd->hqk/dot_general | solution.py:197
  797.7 53.0 %multiply_convert_fusion.9 = bf16[8,512,4096]{2,1,0:T(8,128)(2,1)} fusion(f32[8,512,4096]{2,1,0:T(8,128)} %subtract_exponential_fusion.3, f32[8,512,4096]{2,1,0:T(8,128)} %get-tuple-element.1840, f32[8,512]{1,0:T(8,128)S(1)} %get-tuple-element.1841), kind=kLoop, calls=%fused_computation.38.clone.1 | loop fusion | flops 50331648 | bytes 167788544 | tf_op jit(solution)/shard_map/while/body/eval_jaxpr/while/body/eval_jaxpr/convert_element_type | solution.py:201
  951.8 43.6 %multiply_reduce_fusion.9 = (f32[8,512]{1,0:T(8,128)S(1)}, f32[8,512,4096]{2,1,0:T(8,128)}) fusion(f32[8,512,4096]{2,1,0:T(8,128)} %subtract_exponential_fusion.3, bf16[4096,8,64]{0,2,1:T(8,128)(2,1)S(1)} %copy-done, bf16[1024,8,64]{0,2,1:T(8,128)(2,1)} %get-tuple-element.1924, s32[]{:T(128)S(6)} %select_n.291), kind=kOutput, calls=%fused_computation.39.clone.2 | convolution fusion | flops 2181033984 | bytes 138952704 | tf_op jit(solution)/shard_map/while/body/eval_jaxpr/while/body/eval_jaxpr/qhd,khd->hqk/dot_general | solution.py:197
  995.4 53.0 %multiply_convert_fusion.9 = bf16[8,512,4096]{2,1,0:T(8,128)(2,1)} fusion(f32[8,512,4096]{2,1,0:T(8,128)} %subtract_exponential_fusion.3, f32[8,512,4096]{2,1,0:T(8,128)} %get-tuple-element.1840, f32[8,512]{1,0:T(8,128)S(1)} %get-tuple-element.1841), kind=kLoop, calls=%fused_computation.38.clone.1 | loop fusion | flops 50331648 | bytes 167788544 | tf_op jit(solution)/shard_map/while/body/eval_jaxpr/while/body/eval_jaxpr/convert_element_type | solution.py:201
  1145.3 47.1 %reduce-scatter.23.cloned.1.call-done = bf16[1024,512]{1,0:T(8,128)(2,1)} async-done(((bf16[4096,512]{1,0:T(8,128)(2,1)}), bf16[1024,512]{1,0:T(8,128)(2,1)}) %reduce-scatter.23.cloned.1.call-update) | async-done | bytes 1048592 | tf_op jit(solution)/shard_map/while/body/eval_jaxpr/reduce_scatter | solution.py:226
  1261.4 44.2 %reduce-scatter.27.cloned.1.call-done = f32[512,1024]{1,0:T(8,128)} async-done(((f32[1024,1024]{1,0:T(8,128)}), f32[512,1024]{1,0:T(8,128)}) %reduce-scatter.27.cloned.1.call-update) | async-done | bytes 2097168 | tf_op jit(solution)/shard_map/while/body/eval_jaxpr/reduce_scatter | solution.py:106
  1387.5 56.3 %collective-permute-done.1 = bf16[2048,512]{0,1:T(8,128)(2,1)} collective-permute-done((bf16[2048,512]{0,1:T(8,128)(2,1)}, bf16[2048,512]{0,1:T(8,128)(2,1)}, u32[]{:S(2)}, u32[]{:S(2)}) %collective-permute-start.1) | collective-permute-done | bytes 2097184 | tf_op jit(solution)/shard_map/while/body/eval_jaxpr/ppermute | solution.py:22
  1452.0 166.5 %while.108 = (s32[]{:T(128)}, bf16[2,512,8,64]{1,3,2,0:T(8,128)(2,1)}, f32[2,8,512]{2,1,0:T(8,128)S(1)}, s32[4096]{0:T(1024)S(1)}, s32[2]{0:T(128)S(1)}, /*index...) while((s32[]{:T(128)}, ...), condition=%wide.region_7.7_spmd.clone, body=%wide.region_3.6_spmd.clone.sunk | while | flops 4511079424 | bytes 219897072 | solution.py:152
  1625.6 53.8 %reduce-scatter.19.cloned.1.call-done = f32[512,1024]{1,0:T(8,128)} async-done(((f32[1024,1024]{1,0:T(8,128)}), f32[512,1024]{1,0:T(8,128)}) %reduce-scatter.19.cloned.1.call-update) | async-done | bytes 2097168 | tf_op jit(solution)/shard_map/while/body/eval_jaxpr/reduce_scatter | solution.py:103
  1773.3 54.5 %reduce-scatter.21.cloned.1.call-done = f32[512,1024]{1,0:T(8,128)} async-done(((f32[1024,1024]{1,0:T(8,128)}), f32[512,1024]{1,0:T(8,128)}) %reduce-scatter.21.cloned.1.call-update) | async-done | bytes 2097168 | tf_op jit(solution)/shard_map/while/body/eval_jaxpr/reduce_scatter | solution.py:106
  1873.3 396.0 %while.109 = (s32[]{:T(128)}, f32[4096,8,64]{0,2,1:T(8,128)}, f32[4096,8,64]{0,2,1:T(8,128)}, bf16[2,512,8,64]{1,3,2,0:T(8,128)(2,1)}, s32[2]{0:T(128)S(1)}, /*i...) while((s32[]{:T(128)}, f32[4096,8,64]{0,2,1:T(8,128)}, ...), condition=%wide.region_17.17_spmd.clone.clone, body=%wide.region_14.16_spmd.clone.clone.sunk | while | flops 10913946624 | bytes 590913280 | solution.py:216
  1935.6 43.6 %multiply_reduce_fusion.9 = (f32[8,512]{1,0:T(8,128)S(1)}, f32[8,512,4096]{2,1,0:T(8,128)}) fusion(f32[8,512,4096]{2,1,0:T(8,128)} %subtract_exponential_fusion.3, bf16[4096,8,64]{0,2,1:T(8,128)(2,1)S(1)} %copy-done, bf16[1024,8,64]{0,2,1:T(8,128)(2,1)} %get-tuple-element.1924, s32[]{:T(128)S(6)} %select_n.291), kind=kOutput, calls=%fused_computation.39.clone.2 | convolution fusion | flops 2181033984 | bytes 138952704 | tf_op jit(solution)/shard_map/while/body/eval_jaxpr/while/body/eval_jaxpr/qhd,khd->hqk/dot_general | solution.py:197
  1979.2 53.0 %multiply_convert_fusion.9 = bf16[8,512,4096]{2,1,0:T(8,128)(2,1)} fusion(f32[8,512,4096]{2,1,0:T(8,128)} %subtract_exponential_fusion.3, f32[8,512,4096]{2,1,0:T(8,128)} %get-tuple-element.1840, f32[8,512]{1,0:T(8,128)S(1)} %get-tuple-element.1841), kind=kLoop, calls=%fused_computation.38.clone.1 | loop fusion | flops 50331648 | bytes 167788544 | tf_op jit(solution)/shard_map/while/body/eval_jaxpr/while/body/eval_jaxpr/convert_element_type | solution.py:201
  2176.9 53.0 %multiply_convert_fusion.9 = bf16[8,512,4096]{2,1,0:T(8,128)(2,1)} fusion(f32[8,512,4096]{2,1,0:T(8,128)} %subtract_exponential_fusion.3, f32[8,512,4096]{2,1,0:T(8,128)} %get-tuple-element.1840, f32[8,512]{1,0:T(8,128)S(1)} %get-tuple-element.1841), kind=kLoop, calls=%fused_computation.38.clone.1 | loop fusion | flops 50331648 | bytes 167788544 | tf_op jit(solution)/shard_map/while/body/eval_jaxpr/while/body/eval_jaxpr/convert_element_type | solution.py:201
  2326.6 47.0 %reduce-scatter.23.cloned.1.call-done = bf16[1024,512]{1,0:T(8,128)(2,1)} async-done(((bf16[4096,512]{1,0:T(8,128)(2,1)}), bf16[1024,512]{1,0:T(8,128)(2,1)}) %reduce-scatter.23.cloned.1.call-update) | async-done | bytes 1048592 | tf_op jit(solution)/shard_map/while/body/eval_jaxpr/reduce_scatter | solution.py:226
  2561.9 66.5 %reduce-scatter.11.cloned.1.call-done = bf16[64,3,512]{2,0,1:T(8,128)(2,1)} async-done(((bf16[1024,3,512]{2,0,1:T(8,128)(2,1)}), bf16[64,3,512]{2,0,1:T(8,128)(2,1)}) %reduce-scatter.11.cloned.1.call-update) | async-done | bytes 196624 | tf_op jit(solution)/shard_map/reduce_scatter | solution.py:310
  2630.2 73.9 %reduce-scatter.15.cloned.1.call-done = bf16[64,2048]{1,0:T(8,128)(2,1)} async-done(((bf16[1024,2048]{1,0:T(8,128)(2,1)}), bf16[64,2048]{1,0:T(8,128)(2,1)}) %reduce-scatter.15.cloned.1.call-update) | async-done | bytes 262160 | tf_op jit(solution)/shard_map/reduce_scatter | solution.py:320
  2705.9 73.8 %reduce-scatter.17.cloned.1.call-done = bf16[2048,64]{0,1:T(8,128)(2,1)} async-done(((bf16[2048,1024]{0,1:T(8,128)(2,1)}), bf16[2048,64]{0,1:T(8,128)(2,1)}) %reduce-scatter.17.cloned.1.call-update) | async-done | bytes 262160 | tf_op jit(solution)/shard_map/reduce_scatter | solution.py:324
  (714 shorter events, 1720.7 us)
Async XLA Ops:
  8.7 86.6 %all-gather.24.cloned.1.call-start = ((), (), s32[]{:S(2)}) async-start(), calls=%async_computation.13 | async-start | bytes 5242880 | tf_op jit(solution)/shard_map/all_gather | solution.py:111
  9.4 122.3 %all-gather.20.cloned.1.call-start = ((), (), s32[]{:S(2)}) async-start(), calls=%async_computation.11 | async-start | bytes 5242880 | tf_op jit(solution)/shard_map/all_gather | solution.py:112
  138.8 130.6 %all-gather.28.cloned.1.call-start = ((), (), s32[]{:S(2)}) async-start(), calls=%async_computation.19 | async-start | bytes 5242880 | tf_op jit(solution)/shard_map/while/body/eval_jaxpr/all_gather | solution.py:135
  180.5 317.4 %reduce-scatter.19.cloned.1.call-start = ((), (), s32[]{:S(2)}) async-start(), calls=%async_computation.20 | async-start | bytes 6291456 | tf_op jit(solution)/shard_map/while/body/eval_jaxpr/reduce_scatter | solution.py:103
  444.1 91.1 %all-gather.30.cloned.1.call-start = ((), (), s32[]{:S(2)}) async-start(), calls=%async_computation.21 | async-start | bytes 3145728 | tf_op jit(solution)/shard_map/while/body/eval_jaxpr/all_gather | solution.py:97
  501.9 67.9 %all-gather.32.cloned.1.call-start = ((), (), s32[]{:S(2)}) async-start(), calls=%async_computation.22 | async-start | bytes 3145728 | tf_op jit(solution)/shard_map/while/body/eval_jaxpr/all_gather | solution.py:100
  505.0 141.5 %reduce-scatter.21.cloned.1.call-start = ((), (), s32[]{:S(2)}) async-start(), calls=%async_computation.23 | async-start | bytes 6291456 | tf_op jit(solution)/shard_map/while/body/eval_jaxpr/reduce_scatter | solution.py:106
  592.0 95.0 %all-gather.34.cloned.1.call-start = ((), (), s32[]{:S(2)}) async-start(), calls=%async_computation.24 | async-start | bytes 3145728 | tf_op jit(solution)/shard_map/while/body/eval_jaxpr/all_gather | solution.py:100
  653.7 491.6 %reduce-scatter.25.cloned.1.call-start = ((), (), s32[]{:S(2)}) async-start(), calls=%async_computation.26 | async-start | bytes 5242880 | tf_op jit(solution)/shard_map/while/body/eval_jaxpr/reduce_scatter | solution.py:220
  1100.6 91.9 %reduce-scatter.23.cloned.1.call-start = ((), (), s32[]{:S(2)}) async-start(), calls=%async_computation.25 | async-start | bytes 5242880 | tf_op jit(solution)/shard_map/while/body/eval_jaxpr/reduce_scatter | solution.py:226
  1113.4 135.6 %reduce-scatter.29.cloned.1.call-start = ((), (), s32[]{:S(2)}) async-start(), calls=%async_computation.28 | async-start | bytes 6291456 | tf_op jit(solution)/shard_map/while/body/eval_jaxpr/reduce_scatter | solution.py:103
  1126.1 179.4 %reduce-scatter.27.cloned.1.call-start = ((), (), s32[]{:S(2)}) async-start(), calls=%async_computation.27 | async-start | bytes 6291456 | tf_op jit(solution)/shard_map/while/body/eval_jaxpr/reduce_scatter | solution.py:106
  1320.2 130.7 %all-gather.28.cloned.1.call-start = ((), (), s32[]{:S(2)}) async-start(), calls=%async_computation.19 | async-start | bytes 5242880 | tf_op jit(solution)/shard_map/while/body/eval_jaxpr/all_gather | solution.py:135
  1361.9 317.5 %reduce-scatter.19.cloned.1.call-start = ((), (), s32[]{:S(2)}) async-start(), calls=%async_computation.20 | async-start | bytes 6291456 | tf_op jit(solution)/shard_map/while/body/eval_jaxpr/reduce_scatter | solution.py:103
  1625.5 91.1 %all-gather.30.cloned.1.call-start = ((), (), s32[]{:S(2)}) async-start(), calls=%async_computation.21 | async-start | bytes 3145728 | tf_op jit(solution)/shard_map/while/body/eval_jaxpr/all_gather | solution.py:97
  1686.4 141.4 %reduce-scatter.21.cloned.1.call-start = ((), (), s32[]{:S(2)}) async-start(), calls=%async_computation.23 | async-start | bytes 6291456 | tf_op jit(solution)/shard_map/while/body/eval_jaxpr/reduce_scatter | solution.py:106
  1773.2 95.0 %all-gather.34.cloned.1.call-start = ((), (), s32[]{:S(2)}) async-start(), calls=%async_computation.24 | async-start | bytes 3145728 | tf_op jit(solution)/shard_map/while/body/eval_jaxpr/all_gather | solution.py:100
  1835.0 491.5 %reduce-scatter.25.cloned.1.call-start = ((), (), s32[]{:S(2)}) async-start(), calls=%async_computation.26 | async-start | bytes 5242880 | tf_op jit(solution)/shard_map/while/body/eval_jaxpr/reduce_scatter | solution.py:220
  2281.8 91.7 %reduce-scatter.23.cloned.1.call-start = ((), (), s32[]{:S(2)}) async-start(), calls=%async_computation.25 | async-start | bytes 5242880 | tf_op jit(solution)/shard_map/while/body/eval_jaxpr/reduce_scatter | solution.py:226
  2294.7 135.6 %reduce-scatter.29.cloned.1.call-start = ((), (), s32[]{:S(2)}) async-start(), calls=%async_computation.28 | async-start | bytes 6291456 | tf_op jit(solution)/shard_map/while/body/eval_jaxpr/reduce_scatter | solution.py:103
  2307.4 179.4 %reduce-scatter.27.cloned.1.call-start = ((), (), s32[]{:S(2)}) async-start(), calls=%async_computation.27 | async-start | bytes 6291456 | tf_op jit(solution)/shard_map/while/body/eval_jaxpr/reduce_scatter | solution.py:106
  2500.0 128.5 %reduce-scatter.11.cloned.1.call-start = ((), (), s32[]{:S(2)}) async-start(), calls=%async_computation.14 | async-start | bytes 3342336 | tf_op jit(solution)/shard_map/reduce_scatter | solution.py:310
  2504.9 199.2 %reduce-scatter.15.cloned.1.call-start = ((), (), s32[]{:S(2)}) async-start(), calls=%async_computation.16 | async-start | bytes 4456448 | tf_op jit(solution)/shard_map/reduce_scatter | solution.py:320
  2511.1 268.6 %reduce-scatter.17.cloned.1.call-start = ((), (), s32[]{:S(2)}) async-start(), calls=%async_computation.17 | async-start | bytes 4456448 | tf_op jit(solution)/shard_map/reduce_scatter | solution.py:324
  (200 other events, 4662.1 us)
Sparse Core Ops, SparseCore 0:
  60.8 34.4 all-gather.23
  96.7 34.9 all-gather.19
  138.9 33.0 all-gather.25
  180.6 47.1 all-gather.27
  444.2 53.6 reduce-scatter.18
  502.0 33.0 all-gather.29
  592.1 54.3 reduce-scatter.20
  1100.7 44.5 reduce-scatter.24
  1147.8 44.5 reduce-scatter.22
  1194.6 54.3 reduce-scatter.28
  1251.1 54.3 reduce-scatter.26
  1320.3 33.0 all-gather.25
  1362.0 47.1 all-gather.27
  1625.6 53.6 reduce-scatter.18
  1683.5 33.0 all-gather.29
  1773.4 54.3 reduce-scatter.20
  2282.0 44.5 reduce-scatter.24
  2328.9 44.5 reduce-scatter.22
  2375.8 54.3 reduce-scatter.28
  2432.4 54.3 reduce-scatter.26
  2501.5 57.8 reduce-scatter.12
  2563.1 65.2 reduce-scatter.10
  2632.3 71.7 reduce-scatter.14
  2707.8 71.7 reduce-scatter.16
  (6 shorter events, 180.0 us)
